TPU v7x, 512 devices: a whole 4x8x8 slice. The times are simulated.
512 devices in a mesh: dp: 32 (over y, x_lo, core), mp: 16 (over z, x_hi).
Axes of the slice: x: 4 (x_hi: 2, x_lo: 2; x = x_hi * 2 + x_lo), y: 8, z: 8, core: 2. Of those that a mesh axis runs over, the one named last changes fastest.
Arguments:
- hidden: bfloat16 [4096, 2048], P('dp', 'mp'), may hold values from -6 to 6
- q_weight: bfloat16 [2048, 3072], P('dp', 'mp'), may hold values from -0.125 to 0.125
- dkv_weight: bfloat16 [2048, 576], P('mp', 'dp'), may hold values from -0.125 to 0.125
- latent_gain: float32 [512], replicated, may hold values from 0.1 to 1.9
- kvb_weight: bfloat16 [512, 16, 256], P('dp', 'mp'), may hold values from -0.25 to 0.25
- out_weight: bfloat16 [2048, 2048], P('mp', 'dp'), may hold values from -0.125 to 0.125
- cache: bfloat16 [8192, 64, 576], P(('dp', 'mp')), may hold values from -200 to 200
- cache_len: int32 [64], P('dp'), may hold values from 64 to 8128
- draft_count: int32 [64], P('dp'), may hold values from 32 to 64
- parents: int32 [64, 64], P('dp'), may hold values from 0 to 62, as said below
- accept_node: int32 [64], P('dp'), may hold values from 0 to 63, as said below
- page_table: int32 [64, 128], P('dp'), may hold values from 0 to 255, as said below
Outputs:
- attended: bfloat16 [4096, 2048], P(('dp', 'mp'))
- new_cache: bfloat16 [8192, 64, 576], P(('dp', 'mp'))
Inputs may be any that keep to these rules, and one draw needn't show every extreme that they name: `page_table`: within each group of 2 consecutive requests the entries are a permutation of 0 to 255; entry v is slot v % 16 of the group's device v // 16 along mp. parents[q, 0] = 0 and parents[q, i] < i for i >= 1. `accept_node`: less than the request's draft_count.
All inputs are finite; a program needn't handle non-finite values.
Results may differ from a plain program's by a relative error of at most 0.03.
Values may be sent and summed in bfloat16 or wider, within the bound.
No kernel may reach another device: no remote copies, remote signals or barrier semaphores. Data moves between devices by JAX's collectives and lax.ppermute only.
A program may use at most 64 MiB of HBM per device.

v0:
```python
import jax
import jax.numpy as jnp
from jax import lax
from jax.sharding import PartitionSpec as P

NOPE = 128
ROPE = 64
LAT = 512


def tree_reach(parent_row):
    count = parent_row.shape[0]
    index = jnp.arange(count, dtype=jnp.int32)
    linked = jnp.logical_or(
        parent_row[:, None] == index[None, :], index[:, None] == index[None, :]
    ).astype(jnp.float32)
    for _ in range(max(1, (count - 1).bit_length())):
        linked = jnp.minimum(jnp.dot(linked, linked, precision=lax.Precision.HIGHEST), 1.0)
    return linked


def angles(positions, width):
    half_dim = width // 2
    inverse = 10000.0 ** (-(jnp.arange(half_dim, dtype=jnp.float32) * 2.0) / width)
    phase = positions[..., None] * inverse
    return (jnp.cos(phase), jnp.sin(phase))


def rotary(values, cosine, sine):
    half_dim = values.shape[-1] // 2
    first = values[..., :half_dim]
    second = values[..., half_dim:]
    return jnp.concatenate(
        [first * cosine - second * sine, second * cosine + first * sine], axis=-1
    )


def lookup(index_rows, table):
    choices_hot = index_rows[:, None] == jnp.arange(table.shape[0], dtype=jnp.int32)[None, :]
    return jnp.sum(jnp.where(choices_hot, table[None, :], jnp.zeros((), table.dtype)), axis=1)


def tree_part(q_rows, fresh_req, linked, value_maps, scale_val):
    reqs, draft, heads, width = q_rows.shape
    tree_scores = (
        jnp.einsum("rthc,rjc->rthj", q_rows, fresh_req, preferred_element_type=jnp.float32)
        * scale_val
    )
    tree_live = (linked > 0.5)[:, :, None, :]
    tree_top = jnp.max(jnp.where(tree_live, tree_scores, -1e30), axis=3)
    tree_weights = jnp.where(tree_live, jnp.exp(tree_scores - tree_top[..., None]), 0.0)
    tree_sum = jnp.sum(tree_weights, axis=3).reshape(reqs * draft, heads)
    tree_lat = jnp.einsum(
        "rthj,rjl->rthl",
        tree_weights.astype(jnp.bfloat16),
        fresh_req[..., :LAT],
        preferred_element_type=jnp.float32,
    )
    tree_v = jnp.einsum(
        "thl,lhv->thv",
        tree_lat.reshape(reqs * draft, heads, LAT),
        value_maps.astype(jnp.float32),
        precision=lax.Precision.HIGHEST,
    )
    return (tree_top.reshape(reqs * draft, heads), tree_sum, tree_v)


def joined(cache_top, cache_v, cache_sum, tree_top, tree_sum, tree_v):
    joint = jnp.maximum(cache_top, tree_top)
    left_scale = jnp.exp(cache_top - joint)
    right_scale = jnp.exp(tree_top - joint)
    combined = (cache_v * left_scale[..., None] + tree_v * right_scale[..., None]) / (
        cache_sum * left_scale + tree_sum * right_scale
    )[..., None]
    return combined.astype(jnp.bfloat16).reshape(
        combined.shape[0], combined.shape[1] * combined.shape[2]
    )


def per_device(
    hidden,
    q_weight,
    dkv_weight,
    latent_gain,
    kvb_weight,
    out_weight,
    cache,
    cache_len,
    draft_count,
    parents,
    accept_node,
    page_table,
):
    highest = lax.Precision.HIGHEST
    mp_size = lax.axis_size("mp")
    mp_rank = lax.axis_index("mp")
    reqs, draft = parents.shape
    tokens = reqs * draft
    heads_mine = kvb_weight.shape[1]
    heads_all = heads_mine * mp_size
    slot_count, page_len, width = cache.shape
    scale_val = (NOPE + ROPE) ** (-0.5)
    share = tokens // mp_size
    full_x = lax.all_gather(hidden, "mp", axis=1, tiled=True)
    query = jnp.dot(
        full_x,
        lax.all_gather(q_weight, "dp", axis=0, tiled=True),
        preferred_element_type=jnp.float32,
    )
    query = query.astype(jnp.bfloat16).reshape(tokens, heads_mine, NOPE + ROPE)
    linked = jax.vmap(tree_reach)(parents)
    depth = jnp.sum(linked, axis=2) - 1.0
    positions = (cache_len.astype(jnp.float32)[:, None] + depth).reshape(tokens)
    cosine, sine = angles(positions, ROPE)
    down_cols = lax.all_gather(dkv_weight, "dp", axis=1, tiled=True)
    down_full = lax.all_gather(down_cols, "mp", axis=0, tiled=True)
    compressed = jnp.dot(full_x, down_full, preferred_element_type=jnp.float32)
    latent = compressed[:, :LAT]
    normed = (
        latent * lax.rsqrt(jnp.mean(latent * latent, axis=-1, keepdims=True) + 1e-06) * latent_gain
    )
    fresh = jnp.concatenate([normed, rotary(compressed[:, LAT:], cosine, sine)], axis=-1).astype(
        jnp.bfloat16
    )
    fresh_req = fresh.reshape(reqs, draft, width)
    up_maps = lax.all_gather(kvb_weight, "dp", axis=0, tiled=True)
    q_rope = rotary(query[..., NOPE:].astype(jnp.float32), cosine[:, None, :], sine[:, None, :])
    q_latent = jnp.einsum(
        "thn,lhn->thl", query[..., :NOPE], up_maps[:, :, :NOPE], preferred_element_type=jnp.float32
    )
    mine_abs = jnp.concatenate([q_latent, q_rope], axis=-1).astype(jnp.bfloat16)
    q_all = lax.all_gather(mine_abs, "mp", axis=1, tiled=True)
    value_all = lax.all_gather(up_maps[:, :, NOPE:], "mp", axis=1, tiled=True)
    slot_ids = mp_rank * slot_count + jnp.arange(slot_count, dtype=jnp.int32)
    matched = (page_table[:, :, None] == slot_ids[None, None, :]).astype(jnp.int32)
    slot_req = jnp.sum(matched * jnp.arange(reqs, dtype=jnp.int32)[:, None, None], axis=(0, 1))
    slot_page = jnp.sum(
        matched * jnp.arange(page_table.shape[1], dtype=jnp.int32)[None, :, None], axis=(0, 1)
    )
    key_pos = (
        slot_page[:, None] * page_len + jnp.arange(page_len, dtype=jnp.int32)[None, :]
    ).reshape(slot_count * page_len)
    key_req = jnp.repeat(slot_req, page_len)
    keys = cache.reshape(slot_count * page_len, width)
    top_list = []
    sum_list = []
    out_list = []
    for request in range(reqs):
        rows = q_all[request * draft : (request + 1) * draft].reshape(draft * heads_all, width)
        scores = (
            lax.dot_general(
                rows, keys, (((1,), (1,)), ((), ())), preferred_element_type=jnp.float32
            )
            * scale_val
        )
        live = jnp.logical_and(key_req == request, key_pos < cache_len[request])[None, :]
        top_row = jnp.max(jnp.where(live, scores, -1e30), axis=1)
        weights = jnp.where(live, jnp.exp(scores - top_row[:, None]), 0.0)
        top_list.append(top_row)
        sum_list.append(jnp.sum(weights, axis=1))
        out_list.append(
            jnp.dot(weights.astype(jnp.bfloat16), keys[:, :LAT], preferred_element_type=jnp.float32)
        )
    local_top = jnp.concatenate(top_list).reshape(tokens, heads_all)
    local_sum = jnp.concatenate(sum_list).reshape(tokens, heads_all)
    local_out = jnp.concatenate(out_list, axis=0).reshape(tokens, heads_all, LAT)
    global_top = lax.pmax(local_top, "mp")
    factor = jnp.exp(local_top - global_top)
    partial_v = jnp.einsum(
        "thl,lhv->thv",
        local_out * factor[..., None],
        value_all.astype(jnp.float32),
        precision=highest,
    )
    out_full = lax.all_gather(out_weight, "dp", axis=1, tiled=True)
    row_index = mp_rank * share + jnp.arange(share, dtype=jnp.int32)
    cache_v, cache_sum = (
        lax.psum_scatter(
            partial_v.astype(jnp.bfloat16), "mp", scatter_dimension=1, tiled=True
        ).astype(jnp.float32),
        lax.psum_scatter(
            (local_sum * factor).astype(jnp.bfloat16), "mp", scatter_dimension=1, tiled=True
        ).astype(jnp.float32),
    )
    mine_top = lax.dynamic_slice_in_dim(global_top, mp_rank * heads_mine, heads_mine, 1)
    mine_q = lax.dynamic_slice_in_dim(q_all, mp_rank * heads_mine, heads_mine, 1)
    tree_top, tree_sum, tree_v = tree_part(
        mine_q.reshape(reqs, draft, heads_mine, width),
        fresh_req,
        linked,
        up_maps[:, :, NOPE:],
        scale_val,
    )
    head_out = joined(mine_top, cache_v, cache_sum, tree_top, tree_sum, tree_v)
    mine_rows = lax.psum_scatter(
        jnp.dot(head_out, out_full, preferred_element_type=jnp.float32).astype(jnp.bfloat16),
        "mp",
        scatter_dimension=0,
        tiled=True,
    ).astype(jnp.float32)
    row_count = lookup(row_index // draft, draft_count)
    attended = jnp.where((row_index % draft < row_count)[:, None], mine_rows, 0.0).astype(
        jnp.bfloat16
    )
    accept_hot = (accept_node[:, None] == jnp.arange(draft, dtype=jnp.int32)[None, :]).astype(
        jnp.float32
    )
    path = jnp.einsum("ri,rij->rj", accept_hot, linked, precision=highest)
    deepest = jnp.sum(path, axis=1) - 1.0
    picker = jnp.logical_and(
        path[:, None, :] > 0.5,
        depth[:, None, :] == jnp.arange(draft, dtype=jnp.int32).astype(jnp.float32)[None, :, None],
    )
    entries = jnp.einsum(
        "rdt,rtc->rdc", picker.astype(jnp.bfloat16), fresh_req, preferred_element_type=jnp.float32
    )
    entries = entries.astype(jnp.bfloat16).reshape(tokens, width)
    key_len = lookup(key_req, cache_len)
    key_deep = lookup(key_req, deepest)
    offset = key_pos - key_len
    column = jnp.arange(tokens, dtype=jnp.int32)
    chosen = jnp.logical_and(
        key_req[:, None] == (column // draft)[None, :], offset[:, None] == (column % draft)[None, :]
    )
    chosen = jnp.logical_and(chosen, (offset.astype(jnp.float32) <= key_deep)[:, None])
    placed = jnp.dot(
        chosen.astype(jnp.bfloat16), entries, preferred_element_type=jnp.float32
    ).astype(jnp.bfloat16)
    new_cache = jnp.where(jnp.any(chosen, axis=1)[:, None], placed, keys).reshape(cache.shape)
    return (attended, new_cache)


def solution(mesh):
    return jax.shard_map(
        per_device,
        mesh=mesh,
        in_specs=(
            P("dp", "mp"),
            P("dp", "mp"),
            P("mp", "dp"),
            P(),
            P("dp", "mp", None),
            P("mp", "dp"),
            P(("dp", "mp"), None, None),
            P("dp"),
            P("dp"),
            P("dp", None),
            P("dp"),
            P("dp", None),
        ),
        out_specs=(P(("dp", "mp"), None), P(("dp", "mp"), None, None)),
        check_vma=False,
    )
```

profile of v0, /device:TPU:8, one launch (start us, length us, event | category | flops | bytes accessed | tf_op | source)
XLA Modules:
  0.0 832.7 jit_solution(14350531714993052761)
XLA Ops:
  10.2 50.1 %all_gather.24 = bf16[128,2048]{1,0:T(8,128)(2,1)S(1)} all-gather(bf16[128,128]{1,0:T(8,128)(2,1)} %param.12), channel_id=1, replica_groups=mesh['dp'=32,'mp'=16] {'mp'}, dimensions={1}, use_global_device_ids=true | all-gather | bytes 557056 | tf_op jit(solution)/shard_map/all_gather | solution.py:104
  60.3 34.8 %all_gather.25 = bf16[2048,192]{1,0:T(8,128)(2,1)S(1)} all-gather(bf16[64,192]{1,0:T(8,128)(2,1)} %param.13), channel_id=1, replica_groups=mesh['dp'=32,'mp'=16] {'dp'}, dimensions={0}, use_global_device_ids=true | all-gather | bytes 811008 | tf_op jit(solution)/shard_map/all_gather | solution.py:107
  96.1 31.4 %all_gather.26 = bf16[512,1,256]{2,0,1:T(8,128)(2,1)S(1)} all-gather(bf16[16,1,256]{2,0,1:T(8,128)(2,1)S(1)} %copy-done.8), channel_id=1, replica_groups=mesh['dp'=32,'mp'=16] {'dp'}, dimensions={0}, use_global_device_ids=true | all-gather | bytes 270336 | tf_op jit(solution)/shard_map/all_gather | solution.py:126
  128.6 32.6 %all-gather = bf16[32,18,128]{2,1,0:T(8,128)(2,1)S(1)} all-gather(bf16[1,18,128]{2,1,0:T(8,128)(2,1)S(1)} %bitcast.116), channel_id=1, replica_groups=mesh['dp'=32,'mp'=16] {'dp'}, dimensions={0}, use_global_device_ids=true | all-gather | bytes 152064 | tf_op jit(solution)/shard_map/all_gather | solution.py:115
  164.4 32.7 %all_gather.31 = bf16[128,2048]{0,1:T(8,128)(2,1)S(1)} all-gather(bf16[128,64]{0,1:T(8,128)(2,1)S(1)} %copy-done.7), channel_id=1, replica_groups=mesh['dp'=32,'mp'=16] {'dp'}, dimensions={1}, use_global_device_ids=true | all-gather | bytes 540672 | tf_op jit(solution)/shard_map/all_gather | solution.py:175
  197.2 1.5 copy.98
  202.4 16.0 %all-gather.5.cloned.1.call-done = bf16[128,16,576]{0,2,1:T(8,128)(2,1)} async-done(((bf16[128,1,576]{0,2,1:T(8,128)(2,1)}), bf16[128,16,576]{0,2,1:T(8,128)(2,1)}) %all-gather.5.cloned.1.call-update) | async-done | bytes 2359312 | tf_op jit(solution)/shard_map/all_gather | solution.py:132
  218.4 4.7 fusion.95
  223.1 4.5 copy.85
  227.6 3.4 copy.84
  231.0 5.6 select_reduce_fusion.1
  236.7 5.2 select_reduce_fusion
  241.9 4.5 fusion.1
  247.0 39.1 %pmax.7 = f32[128,16]{0,1:T(8,128)S(1)} all-reduce(f32[128,16]{0,1:T(8,128)S(1)} %pad_maximum_fusion.5), channel_id=1, replica_groups=mesh['dp'=32,'mp'=16] {'mp'}, use_global_device_ids=true, to_apply=%region_6.7 | all-reduce | flops 2048 | bytes 16384 | tf_op jit(solution)/shard_map/pmax | solution.py:167
  286.2 73.8 %all-reduce = bf16[128,16]{1,0:T(8,128)(2,1)S(1)} all-reduce(bf16[128,16]{1,0:T(8,128)(2,1)S(1)} %copy.96), channel_id=3, replica_groups=mesh['dp'=32,'mp'=16] {'mp'}, use_global_device_ids=true, to_apply=%region_12.13.clone | all-reduce | flops 2048 | bytes 8192
  360.1 2.4 fusion.98
  362.8 3.8 fusion.7
  366.6 1.5 fusion.5
  368.0 2.4 pad_maximum_fusion
  370.4 33.0 %all-gather.7.cloned.1.call-done = bf16[512,16,128]{2,0,1:T(8,128)(2,1)} async-done(((bf16[512,1,128]{2,0,1:T(8,128)(2,1)}), bf16[512,16,128]{2,0,1:T(8,128)(2,1)}) %all-gather.7.cloned.1.call-update) | async-done | bytes 2097168 | tf_op jit(solution)/shard_map/all_gather | solution.py:133
  403.4 7.9 fusion.20
  414.8 200.4 %reduce-scatter.4.cloned.1.call-done = bf16[128,1,128]{2,0,1:T(8,128)(2,1)} async-done(((bf16[128,16,128]{2,0,1:T(8,128)(2,1)}), bf16[128,1,128]{2,0,1:T(8,128)(2,1)}) %reduce-scatter.4.cloned.1.call-update) | async-done | bytes 32784 | tf_op jit(solution)/shard_map/reduce_scatter | solution.py:178
  617.6 1.6 fusion.18
  620.6 204.1 %reduce-scatter.6.cloned.1.call-done = bf16[8,2048]{1,0:T(8,128)(2,1)} async-done(((bf16[128,2048]{1,0:T(8,128)(2,1)}), bf16[8,2048]{1,0:T(8,128)(2,1)}) %reduce-scatter.6.cloned.1.call-update) | async-done | bytes 32784 | tf_op jit(solution)/shard_map/reduce_scatter | solution.py:195
  (119 shorter events, 21.6 us)
Async XLA Ops:
  7.2 155.6 %copy-start.10 = (s32[2]{0:T(128)S(1)}, s32[2]{0:T(128)}, u32[]{:S(2)}) copy-start(s32[2]{0:T(128)} %param.19) | copy-start | bytes 28
  7.2 88.9 %copy-start.8 = (bf16[16,1,256]{2,0,1:T(8,128)(2,1)S(1)}, bf16[16,1,256]{2,0,1:T(8,128)(2,1)}, u32[]{:S(2)}) copy-start(bf16[16,1,256]{2,0,1:T(8,128)(2,1)} %param.16) | copy-start | bytes 24580
  7.2 121.4 %copy-start.9 = (bf16[128,18]{0,1:T(8,128)(2,1)S(1)}, bf16[128,18]{0,1:T(8,128)(2,1)}, u32[]{:S(2)}) copy-start(bf16[128,18]{0,1:T(8,128)(2,1)} %param.14) | copy-start | bytes 13828
  7.2 156.2 %copy-start.12 = (s32[2,128]{1,0:T(2,128)S(1)}, s32[2,128]{1,0:T(2,128)}, u32[]{:S(2)}) copy-start(s32[2,128]{1,0:T(2,128)} %param.23) | copy-start | bytes 3076
  7.2 156.5 %copy-start.13 = (s32[2]{0:T(128)S(1)}, s32[2]{0:T(128)}, u32[]{:S(2)}) copy-start(s32[2]{0:T(128)} %param.22) | copy-start | bytes 28
  7.2 157.2 %copy-start.7 = (bf16[128,64]{0,1:T(8,128)(2,1)S(1)}, bf16[128,64]{0,1:T(8,128)(2,1)}, u32[]{:S(2)}) copy-start(bf16[128,64]{0,1:T(8,128)(2,1)} %param.17) | copy-start | bytes 49156
  7.2 190.0 %copy-start.2 = (bf16[16,64,576]{2,1,0:T(8,128)(2,1)S(1)}, bf16[16,64,576]{2,1,0:T(8,128)(2,1)}, u32[]{:S(2)}) copy-start(bf16[16,64,576]{2,1,0:T(8,128)(2,1)} %param.18) | copy-start | bytes 3538948
  7.2 211.2 %all-gather.5.cloned.1.call-start = ((), (), s32[]{:S(2)}) async-start(), calls=%async_computation.2 | async-start | bytes 2506752 | tf_op jit(solution)/shard_map/all_gather | solution.py:132
  60.3 139.6 %copy-start.14 = (s32[2]{0:T(128)S(1)}, s32[2]{0:T(128)}, u32[]{:S(2)}) copy-start(s32[2]{0:T(128)} %param.20) | copy-start | bytes 28
  127.5 74.9 %copy-start.5 = (bf16[512,1,256]{2,0,1:T(8,128)(2,1)}, bf16[512,1,256]{2,0,1:T(8,128)(2,1)S(1)}, u32[]{:S(2)}) copy-start(bf16[512,1,256]{2,0,1:T(8,128)(2,1)S(1)} %all_gather.26) | copy-start | bytes 786436
  128.6 231.5 %all-gather.9.cloned.1.call-start = ((), (), s32[]{:S(2)}) async-start(), calls=%async_computation.5 | async-start | bytes 2506752 | tf_op jit(solution)/shard_map/all_gather | solution.py:116
  161.9 241.5 %all-gather.7.cloned.1.call-start = ((), (), s32[]{:S(2)}) async-start(), calls=%async_computation.3 | async-start | bytes 2228224 | tf_op jit(solution)/shard_map/all_gather | solution.py:133
  162.7 452.4 %reduce-scatter.4.cloned.1.call-start = ((), (), s32[]{:S(2)}) async-start(), calls=%async_computation.4 | async-start | bytes 557056 | tf_op jit(solution)/shard_map/reduce_scatter | solution.py:178
  231.0 5.7 copy-start.1
  241.9 120.8 %copy-start.3 = (bf16[16,64,576]{2,1,0:T(8,128)(2,1)S(1)}, bf16[16,64,576]{2,1,0:T(8,128)(2,1)}, u32[]{:S(2)}) copy-start(bf16[16,64,576]{2,1,0:T(8,128)(2,1)} %param.18) | copy-start | bytes 3538948
  362.8 3.8 copy-start
  370.4 43.1 %copy-start.11 = (f32[512]{0:T(512)S(1)}, f32[512]{0:T(512)}, u32[]{:S(2)}) copy-start(f32[512]{0:T(512)} %param.15) | copy-start | bytes 6148
  403.4 211.7 %copy-start.6 = (bf16[512,1,256]{2,0,1:T(8,128)(2,1)S(1)}, bf16[512,1,256]{2,0,1:T(8,128)(2,1)}, u32[]{:S(2)}) copy-start(bf16[512,1,256]{2,0,1:T(8,128)(2,1)} %copy-done.5) | copy-start | bytes 786436
  411.3 206.2 %copy-start.4 = (bf16[1024,576]{0,1:T(8,128)(2,1)S(1)}, bf16[1024,576]{0,1:T(8,128)(2,1)}, u32[]{:S(2)}) copy-start(bf16[1024,576]{0,1:T(8,128)(2,1)} %copy.98) | copy-start | bytes 3538948
  411.3 413.4 %reduce-scatter.6.cloned.1.call-start = ((), (), s32[]{:S(2)}) async-start(), calls=%async_computation.6 | async-start | bytes 557056 | tf_op jit(solution)/shard_map/reduce_scatter | solution.py:195
Sparse Core Ops, SparseCore 0:
  128.7 89.6 all-gather.4
  221.4 90.6 all-gather.8
  315.3 88.0 all-gather.6
  411.5 203.6 reduce-scatter.3
  620.0 204.7 reduce-scatter.5
where the time goes:
time: 833 us
  waiting for transfers between devices  454 us (55%)
  blocking collectives  294 us (35%)
  matrix products  33.8 us (4%)
  local copies, waits for them, and re-layouts  23.3 us (3%)
  between operations  14.2 us (2%)
  other arithmetic  13.2 us (2%)
    reduce_scatter x1, waiting for transfers between devices, per_device(): lax.psum_scatter(jnp.dot(head_out, out_full, preferred_element_type=jnp.f...  204 us
    reduce_scatter x1, waiting for transfers between devices, per_device(): lax.psum_scatter(partial_v.astype(jnp.bfloat16), 'mp', scatter_dimension=...  200 us
    unnamed x1, blocking collectives  73.8 us
    all_gather x1, blocking collectives, per_device(): full_x = lax.all_gather(hidden, 'mp', axis=1, tiled=True)  50.1 us
    pmax x1, blocking collectives, per_device(): global_top = lax.pmax(local_top, 'mp')  39.1 us
    all_gather x1, blocking collectives, per_device(): lax.all_gather(q_weight, 'dp', axis=0, tiled=True)  34.8 us
    all_gather x1, waiting for transfers between devices, per_device(): value_all = lax.all_gather(up_maps[:, :, NOPE:], 'mp', axis=1, tiled=True)  33 us
    all_gather x1, blocking collectives, per_device(): out_full = lax.all_gather(out_weight, 'dp', axis=1, tiled=True)  32.7 us
  transfers between devices with their start and end apart: 5, of which 4 were waited for; matrix products, arithmetic and copies ran while one was open for 6% of the time, Pallas kernels for 0%

commit v1 on v0

--- a/solution.py
+++ b/solution.py
@@ -6,6 +6,15 @@
 NOPE = 128
 ROPE = 64
 LAT = 512
+
+
+def column_trace(target, mesh_ax="dp"):
+    return jnp.concatenate(
+        jax.lax.all_to_all(
+            jnp.stack(tuple((target for _ in range(jax.lax.axis_size(mesh_ax))))), mesh_ax, 0, 0
+        ),
+        axis=0,
+    )
 
 
 def tree_reach(parent_row):
@@ -102,11 +111,7 @@
     scale_val = (NOPE + ROPE) ** (-0.5)
     share = tokens // mp_size
     full_x = lax.all_gather(hidden, "mp", axis=1, tiled=True)
-    query = jnp.dot(
-        full_x,
-        lax.all_gather(q_weight, "dp", axis=0, tiled=True),
-        preferred_element_type=jnp.float32,
-    )
+    query = jnp.dot(full_x, column_trace(q_weight), preferred_element_type=jnp.float32)
     query = query.astype(jnp.bfloat16).reshape(tokens, heads_mine, NOPE + ROPE)
     linked = jax.vmap(tree_reach)(parents)
     depth = jnp.sum(linked, axis=2) - 1.0

time: 833 us -> 765 us (0.918)
  waiting for transfers between devices: 454 us -> 394 us
  blocking collectives: 294 us -> 276 us
    reduce_scatter x1, waiting for transfers between devices: 200 us -> 127 us  [per_device(): lax.psum_scatter(partial_v.astype(jnp.bfloat16), 'mp', scatter_dimension=...]
    all_gather x1 -> x0, blocking collectives: 34.8 us -> none  [per_device(): lax.all_gather(q_weight, 'dp', axis=0, tiled=True)]
    all_gather x1, waiting for transfers between devices: 16 us -> 46.8 us  [per_device(): q_all = lax.all_gather(mine_abs, 'mp', axis=1, tiled=True)]
    all_gather x1, waiting for transfers between devices: 33 us -> 16.1 us  [per_device(): value_all = lax.all_gather(up_maps[:, :, NOPE:], 'mp', axis=1, tiled=True)]
    all_gather x1, blocking collectives: 31.4 us -> 46.2 us  [per_device(): up_maps = lax.all_gather(kvb_weight, 'dp', axis=0, tiled=True)]
  transfers between devices with their start and end apart: 5 -> 6, of which waited for: 4 -> 4; matrix products, arithmetic and copies ran while one was open for 6% -> 8% of each run, Pallas kernels for 0% -> 0%
where the time goes in v1:
time: 765 us; the launch traced here: 764 us
  waiting for transfers between devices  394 us (52%)
  blocking collectives  276 us (36%)
  matrix products  33.7 us (4%)
  local copies, waits for them, and re-layouts  26.1 us (3%)
  between operations  14.1 us (2%)
  other arithmetic  13.8 us (2%)
    reduce_scatter x1, waiting for transfers between devices, per_device(): lax.psum_scatter(jnp.dot(head_out, out_full, preferred_element_type=jnp.f...  204 us
    reduce_scatter x1, waiting for transfers between devices, per_device(): lax.psum_scatter(partial_v.astype(jnp.bfloat16), 'mp', scatter_dimension=...  127 us
    unnamed x1, blocking collectives  73.2 us
    all_gather x1, blocking collectives, per_device(): full_x = lax.all_gather(hidden, 'mp', axis=1, tiled=True)  50.6 us
    all_gather x1, waiting for transfers between devices, per_device(): q_all = lax.all_gather(mine_abs, 'mp', axis=1, tiled=True)  46.8 us
    all_gather x1, blocking collectives, per_device(): up_maps = lax.all_gather(kvb_weight, 'dp', axis=0, tiled=True)  46.2 us
    pmax x1, blocking collectives, per_device(): global_top = lax.pmax(local_top, 'mp')  39.1 us
    all_gather x1, blocking collectives, per_device(): down_cols = lax.all_gather(dkv_weight, 'dp', axis=1, tiled=True)  34.4 us
  transfers between devices with their start and end apart: 6, of which 4 were waited for; matrix products, arithmetic and copies ran while one was open for 8% of the time, Pallas kernels for 0%

profile of v1, /device:TPU:8, one launch (start us, length us, event | category | flops | bytes accessed | tf_op | source)
XLA Modules:
  0.0 764.1 jit_solution(12952726337259196874)
XLA Ops:
  7.2 34.4 %all-gather = bf16[32,18,128]{2,1,0:T(8,128)(2,1)S(1)} all-gather(bf16[1,18,128]{2,1,0:T(8,128)(2,1)} %bitcast.118), channel_id=1, replica_groups=mesh['dp'=32,'mp'=16] {'dp'}, dimensions={0}, use_global_device_ids=true | all-gather | bytes 152064 | tf_op jit(solution)/shard_map/all_gather | solution.py:120
  42.4 1.9 stack.2
  44.2 6.3 all-to-all-start
  53.5 46.2 %all_gather.22 = bf16[512,1,256]{2,0,1:T(8,128)(2,1)S(1)} all-gather(bf16[16,1,256]{2,0,1:T(8,128)(2,1)S(1)} %copy-done.7), channel_id=1, replica_groups=mesh['dp'=32,'mp'=16] {'dp'}, dimensions={0}, use_global_device_ids=true | all-gather | bytes 270336 | tf_op jit(solution)/shard_map/all_gather | solution.py:131
  99.7 50.6 %all_gather.21 = bf16[128,2048]{1,0:T(8,128)(2,1)S(1)} all-gather(bf16[128,128]{1,0:T(8,128)(2,1)S(1)} %copy-done.5), channel_id=1, replica_groups=mesh['dp'=32,'mp'=16] {'mp'}, dimensions={1}, use_global_device_ids=true | all-gather | bytes 557056 | tf_op jit(solution)/shard_map/all_gather | solution.py:113
  154.8 32.2 %all_gather.27 = bf16[128,2048]{0,1:T(8,128)(2,1)S(1)} all-gather(bf16[128,64]{0,1:T(8,128)(2,1)S(1)} %copy-done.6), channel_id=1, replica_groups=mesh['dp'=32,'mp'=16] {'dp'}, dimensions={1}, use_global_device_ids=true | all-gather | bytes 540672 | tf_op jit(solution)/shard_map/all_gather | solution.py:180
  187.0 2.4 copy.98
  193.2 2.4 fusion.98
  196.5 46.8 %all-gather.5.cloned.1.call-done = bf16[128,16,576]{0,2,1:T(8,128)(2,1)} async-done(((bf16[128,1,576]{0,2,1:T(8,128)(2,1)}), bf16[128,16,576]{0,2,1:T(8,128)(2,1)}) %all-gather.5.cloned.1.call-update) | async-done | bytes 2359312 | tf_op jit(solution)/shard_map/all_gather | solution.py:137
  243.3 4.7 fusion.95
  248.0 4.5 copy.85
  252.5 3.4 copy.84
  255.9 5.6 select_reduce_fusion.1
  261.6 5.1 select_reduce_fusion
  266.9 4.5 fusion.1
  271.9 39.1 %pmax.7 = f32[128,16]{0,1:T(8,128)S(1)} all-reduce(f32[128,16]{0,1:T(8,128)S(1)} %pad_maximum_fusion.5), channel_id=1, replica_groups=mesh['dp'=32,'mp'=16] {'mp'}, use_global_device_ids=true, to_apply=%region_6.7 | all-reduce | flops 2048 | bytes 16384 | tf_op jit(solution)/shard_map/pmax | solution.py:172
  311.1 3.8 fusion.7
  316.4 2.4 pad_maximum_fusion
  318.7 16.1 %all-gather.7.cloned.1.call-done = bf16[512,16,128]{2,0,1:T(8,128)(2,1)} async-done(((bf16[512,1,128]{2,0,1:T(8,128)(2,1)}), bf16[512,16,128]{2,0,1:T(8,128)(2,1)}) %all-gather.7.cloned.1.call-update) | async-done | bytes 2097168 | tf_op jit(solution)/shard_map/all_gather | solution.py:138
  334.8 7.8 %fusion.20 = bf16[128,16,128]{2,0,1:T(8,128)(2,1)} fusion(bf16[512,16,128]{2,0,1:T(8,128)(2,1)} %all-gather.7.cloned.1.call-done, f32[128,16,512]{2,1,0:T(8,128)} %bitcast.98, f32[128,16]{0,1:T(8,128)S(1)} %get-tuple-element.12), kind=kOutput, calls=%fused_computation.26 | convolution fusion | flops 1611923456 | bytes 6823936 | tf_op jit(solution)/shard_map/thl,lhv->thv/dot_general | solution.py:174
  343.4 73.2 %all-reduce = bf16[128,16]{1,0:T(8,128)(2,1)S(1)} all-reduce(bf16[128,16]{1,0:T(8,128)(2,1)S(1)} %copy.96), channel_id=3, replica_groups=mesh['dp'=32,'mp'=16] {'mp'}, use_global_device_ids=true, to_apply=%region_12.13.clone | all-reduce | flops 2048 | bytes 8192
  419.4 127.0 %reduce-scatter.4.cloned.1.call-done = bf16[128,1,128]{2,0,1:T(8,128)(2,1)} async-done(((bf16[128,16,128]{2,0,1:T(8,128)(2,1)}), bf16[128,1,128]{2,0,1:T(8,128)(2,1)}) %reduce-scatter.4.cloned.1.call-update) | async-done | bytes 32784 | tf_op jit(solution)/shard_map/reduce_scatter | solution.py:183
  548.8 1.6 fusion.18
  551.9 204.2 %reduce-scatter.6.cloned.1.call-done = bf16[8,2048]{1,0:T(8,128)(2,1)} async-done(((bf16[128,2048]{1,0:T(8,128)(2,1)}), bf16[8,2048]{1,0:T(8,128)(2,1)}) %reduce-scatter.6.cloned.1.call-update) | async-done | bytes 32784 | tf_op jit(solution)/shard_map/reduce_scatter | solution.py:200
  (117 shorter events, 23.7 us)
Async XLA Ops:
  7.2 46.3 %copy-start.7 = (bf16[16,1,256]{2,0,1:T(8,128)(2,1)S(1)}, bf16[16,1,256]{2,0,1:T(8,128)(2,1)}, u32[]{:S(2)}) copy-start(bf16[16,1,256]{2,0,1:T(8,128)(2,1)} %param.16) | copy-start | bytes 24580
  7.2 92.5 %copy-start.5 = (bf16[128,128]{1,0:T(8,128)(2,1)S(1)}, bf16[128,128]{1,0:T(8,128)(2,1)}, u32[]{:S(2)}) copy-start(bf16[128,128]{1,0:T(8,128)(2,1)} %param.12) | copy-start | bytes 98308
  7.2 186.0 %all-gather.9.cloned.1.call-start = ((), (), s32[]{:S(2)}) async-start(), calls=%async_computation.6 | async-start | bytes 2506752 | tf_op jit(solution)/shard_map/all_gather | solution.py:121
  42.3 110.8 %copy-start.8 = (s32[2]{0:T(128)S(1)}, s32[2]{0:T(128)}, u32[]{:S(2)}) copy-start(s32[2]{0:T(128)} %param.19) | copy-start | bytes 28
  42.3 111.4 %copy-start.10 = (s32[2,128]{1,0:T(2,128)S(1)}, s32[2,128]{1,0:T(2,128)}, u32[]{:S(2)}) copy-start(s32[2,128]{1,0:T(2,128)} %param.23) | copy-start | bytes 3076
  42.4 111.7 %copy-start.11 = (s32[2]{0:T(128)S(1)}, s32[2]{0:T(128)}, u32[]{:S(2)}) copy-start(s32[2]{0:T(128)} %param.22) | copy-start | bytes 28
  42.4 112.4 %copy-start.6 = (bf16[128,64]{0,1:T(8,128)(2,1)S(1)}, bf16[128,64]{0,1:T(8,128)(2,1)}, u32[]{:S(2)}) copy-start(bf16[128,64]{0,1:T(8,128)(2,1)} %param.17) | copy-start | bytes 49156
  44.2 106.0 %all-to-all-start = ((bf16[32,64,192]{2,1,0:T(8,128)(2,1)}), bf16[32,64,192]{2,1,0:T(8,128)(2,1)S(1)}, u32[]{:S(2)}, u32[]{:S(2)}) async-start(bf16[32,64,192]{2,1,0:T(8,128)(2,1)} %stack.2), calls=%async_computation | async-start | bytes 2097152 | tf_op jit(solution)/shard_map/all_to_all | solution.py:13
  50.5 192.8 %all-gather.5.cloned.1.call-start = ((), (), s32[]{:S(2)}) async-start(), calls=%async_computation.3 | async-start | bytes 2506752 | tf_op jit(solution)/shard_map/all_gather | solution.py:137
  52.2 138.5 %copy-start.12 = (s32[2]{0:T(128)S(1)}, s32[2]{0:T(128)}, u32[]{:S(2)}) copy-start(s32[2]{0:T(128)} %param.20) | copy-start | bytes 28
  151.0 44.8 %copy-start.9 = (f32[512]{0:T(512)S(1)}, f32[512]{0:T(512)}, u32[]{:S(2)}) copy-start(f32[512]{0:T(512)} %param.15) | copy-start | bytes 6148
  152.3 182.5 %all-gather.7.cloned.1.call-start = ((), (), s32[]{:S(2)}) async-start(), calls=%async_computation.4 | async-start | bytes 2228224 | tf_op jit(solution)/shard_map/all_gather | solution.py:138
  153.1 393.3 %reduce-scatter.4.cloned.1.call-start = ((), (), s32[]{:S(2)}) async-start(), calls=%async_computation.5 | async-start | bytes 557056 | tf_op jit(solution)/shard_map/reduce_scatter | solution.py:183
  255.9 5.7 copy-start.1
  266.9 44.2 %copy-start.2 = (bf16[16,64,576]{2,1,0:T(8,128)(2,1)S(1)}, bf16[16,64,576]{2,1,0:T(8,128)(2,1)}, u32[]{:S(2)}) copy-start(bf16[16,64,576]{2,1,0:T(8,128)(2,1)} %param.18) | copy-start | bytes 3538948
  311.1 3.8 copy-start
  318.7 24.4 %copy-start.4 = (bf16[128,512]{0,1:T(8,128)(2,1)S(1)}, bf16[128,512]{0,1:T(8,128)(2,1)}, u32[]{:S(2)}) copy-start(bf16[128,512]{0,1:T(8,128)(2,1)} %multiply_convert_fusion) | copy-start | bytes 393220
  342.7 206.2 %copy-start.3 = (bf16[1024,576]{0,1:T(8,128)(2,1)S(1)}, bf16[1024,576]{0,1:T(8,128)(2,1)}, u32[]{:S(2)}) copy-start(bf16[1024,576]{0,1:T(8,128)(2,1)} %copy.98) | copy-start | bytes 3538948
  342.7 413.4 %reduce-scatter.6.cloned.1.call-start = ((), (), s32[]{:S(2)}) async-start(), calls=%async_computation.7 | async-start | bytes 557056 | tf_op jit(solution)/shard_map/reduce_scatter | solution.py:200
Sparse Core Ops, SparseCore 0:
  42.5 102.6 all-gather.8
  152.4 90.8 all-gather.4
  246.5 88.2 all-gather.6
  342.8 203.5 reduce-scatter.3
  551.3 204.7 reduce-scatter.5
